TPU v7x, 256 devices: a whole 4x4x8 slice. The times are simulated.
256 devices in a mesh: row: 32 (over x, z), col: 8 (over y, core).
Axes of the slice: x: 4, y: 4, z: 8, core: 2. Of those that a mesh axis runs over, the one named last changes fastest.
Arguments:
- latent: bfloat16 [1024, 1024, 128], P('row', 'col'), may hold values from -140 to 140
- group_norm_gain: float32 [128], replicated, may hold values from 0.25 to 1.75
- group_norm_bias: float32 [128], replicated, may hold values from -2.5 to 2.5
- decoder_weight: bfloat16 [3, 3, 128, 3], replicated, may hold values from -0.1875 to 0.1875
- decoder_bias: float32 [3], replicated, may hold values from -2.5 to 2.5
- first_weight: bfloat16 [3, 3, 3, 64], replicated, may hold values from -1.25 to 1.25
- first_bias: float32 [64], replicated, may hold values from -2.5 to 2.5
- second_weight: bfloat16 [3, 3, 64, 64], replicated, may hold values from -0.25 to 0.25
- second_bias: float32 [64], replicated, may hold values from -2.5 to 2.5
- third_weight: bfloat16 [3, 3, 64, 128], replicated, may hold values from -0.25 to 0.25
- third_bias: float32 [128], replicated, may hold values from -2.5 to 2.5
- fourth_weight: bfloat16 [3, 3, 128, 128], replicated, may hold values from -0.1875 to 0.1875
- fourth_bias: float32 [128], replicated, may hold values from -2.5 to 2.5
- exemplar_low: float32 [64, 64], replicated, may hold values from -1.2 to 1.2
- exemplar_high: float32 [128, 128], replicated, may hold values from -1.2 to 1.2
Outputs:
- latent_grad: bfloat16 [1024, 1024, 128], P('row', 'col')
- style_loss: float32 [], replicated
All inputs are finite; a program needn't handle non-finite values.
Results may differ from a plain program's by a relative error of at most 0.014.
Values may be sent and summed in bfloat16 or wider, within the bound.
No kernel may reach another device: no remote copies, remote signals or barrier semaphores. Data moves between devices by JAX's collectives and lax.ppermute only.
A program may use at most 64 MiB of HBM per device.

v0:
```python
import jax
import jax.numpy as jnp
import numpy as np
from jax import lax
from jax.experimental import pallas as pl
from jax.experimental.pallas import tpu as pltpu
from jax.sharding import PartitionSpec as P

GROUPS = 32
EPS = 1e-05
PIX_MEAN = (0.485, 0.456, 0.406)
PIX_STD = (0.229, 0.224, 0.225)
HALO = 16
F32 = jnp.float32
BF16 = jnp.bfloat16
INTERPRET = False
VMEM_LIMIT = 40 * 1024 * 1024


def narrow_tables():
    out_fwd = np.zeros((2, 3, 3, 2, 4, 3, 3, 4), np.float32)
    out_bwd = np.zeros_like(out_fwd)
    in_fwd = np.zeros((2, 3, 3, 2, 4, 3, 3, 4), np.float32)
    in_bwd = np.zeros_like(in_fwd)
    for k, s in enumerate((0, -1, 1)):
        for dx in range(3):
            for q in range(2):
                for i in range(2):
                    dy = i - q - 2 * s + 1
                    if 0 <= dy < 3:
                        for c in range(3):
                            out_fwd[i, k, dx, q, c, dy, dx, c] = 1
                            out_bwd[i, k, dx, q, c, 2 - dy, 2 - dx, c] = 1
    for k, s in enumerate((-1, 0, 1)):
        for dx in range(3):
            for q in range(2):
                for i in range(2):
                    dy = 2 * s + i - q + 1
                    if 0 <= dy < 3:
                        for c in range(3):
                            in_fwd[q, k, dx, i, c, dy, dx, c] = 1
                            in_bwd[q, k, dx, i, c, 2 - dy, 2 - dx, c] = 1
    outs = np.concatenate([out_fwd.reshape(2, 72, 36), out_bwd.reshape(2, 72, 36)], 0)
    ins = np.concatenate([in_fwd.reshape(2, 3, 24, 36), in_bwd.reshape(2, 3, 24, 36)], 0)
    ins = np.pad(ins, ((0, 0), (0, 0), (0, 8), (0, 0))).reshape(4, 96, 36)
    return jnp.asarray(outs, BF16), jnp.asarray(ins, BF16)


def weights_kernel(dec, fst, w2r, w3r, w4r, outs, ins, wd, w1, w2, w3, w4, w4t, w3t, w2t, w1t, wdt):
    d, f = dec[...], fst[...]

    def place(t, x):
        return jnp.dot(t, x, preferred_element_type=F32)

    for i in range(2):
        wd[:, i * 128 : (i + 1) * 128] = place(outs[i], d).astype(BF16)
        wdt[:, i * 128 : (i + 1) * 128] = place(ins[2 + i], d).astype(BF16)
    w1[...] = jnp.concatenate([place(ins[0], f), place(ins[1], f)], axis=1).astype(BF16)
    w1t[...] = jnp.concatenate([place(outs[2], f), place(outs[3], f)], axis=1).astype(BF16)

    def tap(w, dy, dx, rows, cols):
        return w[dy, dx] if 0 <= dy < 3 else jnp.zeros((rows, cols), BF16)

    for k, j in enumerate((1, 2, 3, 0)):
        for dx in range(3):
            pair = [tap(w2r, j - q, dx, 64, 64) for q in range(2)]
            w2[k * 64 : (k + 1) * 64, dx * 128 : (dx + 1) * 128] = jnp.concatenate(pair, axis=1)
            pair = [tap(w2r, 2 - j + q, 2 - dx, 64, 64) for q in range(2)]
            w2t[k * 64 : (k + 1) * 64, dx * 128 : (dx + 1) * 128] = jnp.concatenate(pair, axis=0).T
            for q in range(2):
                at = dx * 256 + q * 128
                w3[k * 64 : (k + 1) * 64, at : at + 128] = tap(w3r, j - q, dx, 64, 128)
    for j in range(4):
        for dx in range(3):
            pair = [tap(w3r, 2 - j + q, 2 - dx, 64, 128) for q in range(2)]
            w3t[j * 128 : (j + 1) * 128, dx * 128 : (dx + 1) * 128] = jnp.concatenate(pair, axis=0).T
            for q in range(2):
                at = dx * 256 + q * 128
                w4[j * 128 : (j + 1) * 128, at : at + 128] = tap(w4r, j - q, dx, 128, 128)
                w4t[j * 128 : (j + 1) * 128, at : at + 128] = tap(w4r, 2 - j + q, 2 - dx, 128, 128).T


def iota(shape, axis):
    return lax.broadcasted_iota(jnp.int32, shape, axis)


def split3(x):
    hi = x.astype(BF16).astype(F32)
    mid = (x - hi).astype(BF16).astype(F32)
    lo = x - hi - mid
    r = iota((16, 128), 0)
    return jnp.where(r == 0, hi, jnp.where(r == 1, mid, jnp.where(r == 2, lo, 0.0))).astype(BF16)


def exact_dot(x, table):
    return jnp.sum(jnp.dot(split3(x), table, preferred_element_type=F32), axis=0, keepdims=True)


def group_rows(s, q):
    c = iota((128, 128), 0) // (128 // GROUPS)
    l = iota((128, 128), 1)
    g1 = jnp.where(l == c, 1.0, 0.0).astype(BF16)
    g2 = jnp.where(l == c + GROUPS, 1.0, 0.0).astype(BF16)
    s = jnp.sum(s, axis=0, keepdims=True)
    q = jnp.sum(q, axis=0, keepdims=True)
    return exact_dot(s, g1) + exact_dot(q, g2)


def group_values(rows, count):
    tot = jnp.sum(rows, axis=0, keepdims=True)
    l = iota((128, 256), 0)
    c = iota((128, 256), 1)
    want = (c % 128) // (128 // GROUPS) + GROUPS * (c // 128)
    e = jnp.where(l == want, 1.0, 0.0).astype(BF16)
    v = exact_dot(tot, e) * (1.0 / count)
    return v[:, 0:128], v[:, 128:256]


def norm_values(rows, count):
    mean, msq = group_values(rows, count)
    return mean, lax.rsqrt(msq - mean * mean + EPS)


def gelu_both(a):
    e = jnp.exp2(a * a * (-0.5 * 1.4426950408889634))
    t = 1.0 / (1.0 + jnp.abs(a) * (0.3275911 * 0.7071067811865476))
    poly = 0.5 * -1.453152027 + t * (0.5 * 1.061405429)
    poly = 0.5 * 1.421413741 + t * poly
    poly = 0.5 * -0.284496736 + t * poly
    q = t * (0.5 * 0.254829592 + t * poly) * e
    phi = jnp.where(a >= 0.0, 1.0 - q, q)
    return a * phi, phi + (a * 0.3989422804014327) * e


def pipelined(n, product, use, bufs):
    a, b = bufs
    product(0, a)
    steps = (n - 1) // 2

    def body(i):
        g = 2 * i
        product(g + 1, b)
        use(g, a)
        product(g + 2, a)
        use(g + 1, b)

    loop(0, steps, body)
    if n % 2 == 0:
        product(n - 1, b)
        use(n - 2, a)
        use(n - 1, b)
    else:
        use(n - 1, a)


def store_product(buf, x, w):
    m, n = x.shape[0], w.shape[1]
    buf[8 : 8 + m, 0:n] = jnp.dot(x, w, preferred_element_type=F32)
    buf[8 + m : 16 + m, 0:n] = jnp.zeros((8, n), F32)


def both_halves(own, near, start, n):
    m, lanes = n * own.shape[1], own.shape[2]
    return jnp.concatenate(
        [own[pl.ds(start, n)].reshape(m, lanes), near[pl.ds(start, n)].reshape(m, lanes)], axis=1
    )


def taps(buf, start, size, n, at=0, width=None):
    width = n if width is None else width
    lo = 8 + start
    return (
        buf[lo : lo + size, n + at : n + at + width]
        + buf[lo - 1 : lo - 1 + size, at : at + width]
        + buf[lo + 1 : lo + 1 + size, 2 * n + at : 2 * n + at + width]
    )


def lane_taps(c):
    return pltpu.roll(c[0:8], 1, 1) + c[8:16] + pltpu.roll(c[16:24], 255, 1)


def nt(a, b):
    return lax.dot_general(a, b, (((1,), (1,)), ((), ())), preferred_element_type=F32)


def tn(a, b):
    return lax.dot_general(a, b, (((0,), (0,)), ((), ())), preferred_element_type=F32)


def loop(lo, hi, body):
    lax.fori_loop(lo, hi, lambda i, c: (body(i), c)[1], 0)


def color_column(values):
    c = iota((8, 1), 0) % 4
    out = jnp.zeros((8, 1), F32)
    for k, v in enumerate(values):
        out = jnp.where(c == k, v, out)
    return out


def stats_kernel(n, x_ref, o_ref):
    x_ref = x_ref.ready()
    rows, cols, channels = x_ref.shape

    def body(r, carry):
        s, q = carry
        for i in range(4):
            x = x_ref[4 * r + i].astype(F32).reshape(cols // 8, 8, channels)
            s = s + jnp.sum(x, axis=0)
            q = q + jnp.sum(x * x, axis=0)
        return s, q

    z = jnp.zeros((8, channels), F32)
    s, q = lax.fori_loop(0, rows // 4, body, (z, z))
    o_ref[...] = jnp.broadcast_to(group_rows(s, q), (n, 128))


def slab_kernel(x, up, down, right, left, sems):
    rows, cols, _ = x.shape
    h = HALO
    copies = []
    for out, at in ((right, cols - h), (left, 0)):
        for src, r in ((up, 0), (x, h), (down, h + rows)):
            k = len(copies)
            dst = out.at[pl.ds(r, src.shape[0])]
            copies.append(pltpu.make_async_copy(src.at[:, pl.ds(at, h)], dst, sems.at[k]))
            copies[-1].start()
    for c in copies:
        c.wait()


def forward_kernel(
    dims,
    idx,
    dbias,
    lat_hbm,
    up,
    down,
    left,
    right,
    stats,
    vecs,
    wd,
    w1,
    w2,
    w3,
    w4,
    gram,
    norm,
    o_slope1,
    o_feat2,
    o_slope2,
    o_slope3,
    o_feat4,
    o_slope4,
    o_sact,
    lat,
    tt,
    pixcol,
    y1,
    y1n,
    yp,
    ypn,
    pool,
    f3,
    fm,
    cm,
    hm,
    om,
    pa,
    pb,
    sems,
):
    rows, cols, image_rows, image_cols, count = dims
    h = HALO
    width = cols + 2 * h
    half = width // 2
    pairs = (rows + 2 * h) // 2
    pieces = (
        (lat_hbm, lat.at[pl.ds(h, rows), pl.ds(h, cols)]),
        (up, lat.at[pl.ds(0, h), pl.ds(h, cols)]),
        (down, lat.at[pl.ds(h + rows, h), pl.ds(h, cols)]),
        (left, lat.at[:, pl.ds(0, h)]),
        (right, lat.at[:, pl.ds(h + cols, h)]),
    )
    copies = [pltpu.make_async_copy(a, b, sems.at[i]) for i, (a, b) in enumerate(pieces)]
    for c in copies:
        c.start()
    slope1, feat2, slope2, slope3 = o_slope1.ref, o_feat2.ref, o_slope2.ref, o_slope3.ref
    feat4, slope4, sact = o_feat4.ref, o_slope4.ref, o_sact.ref

    pa[0:8] = jnp.zeros((8, pa.shape[1]), F32)
    pb[0:8] = jnp.zeros((8, pb.shape[1]), F32)
    tt[:, :, 128:256] = jnp.zeros((pairs, 72, 128), F32)
    pixcol[0] = jnp.zeros((32, 256), BF16)
    pixcol[pairs - 1] = jnp.zeros((32, 256), BF16)
    ypn[1, :, 64:128] = jnp.zeros((half, 64), BF16)
    ypn[pairs // 2 - 2, :, 0:64] = jnp.zeros((half, 64), BF16)

    row0 = idx[0] * rows - h
    col0 = idx[1] * cols - h

    def valid_rows(r):
        return jnp.where((row0 + r >= 0) & (row0 + r < image_rows), 1.0, 0.0).astype(F32)

    def valid_lanes(r):
        return jnp.full((1, 128), valid_rows(r), F32).astype(BF16)

    def col_mask(n, step, lanes):
        c = col0 + step * iota((n, lanes), 0)
        return jnp.where((c >= 0) & (c < image_cols), 1.0, 0.0).astype(BF16)

    cm[...] = col_mask(width, 1, 128)
    hm[...] = col_mask(half, 2, 128)
    own = iota((half, 128), 0)
    om[...] = jnp.where((own >= h // 2) & (own < h // 2 + cols // 2), 1.0, 0.0).astype(BF16)
    lane = iota((8, 256), 1)
    lmask = jnp.where((col0 + lane >= 0) & (col0 + lane < image_cols) & (lane < width), 1.0, 0.0)
    lmask = lmask.astype(F32)

    mean, rstd = norm_values(stats[...], count)
    norm[0:1] = mean
    norm[1:2] = rstd
    gain = vecs[0:1]
    scale = rstd * gain
    shift = vecs[1:2] - mean * scale
    b1, b2, b3, b4 = vecs[2:3], vecs[3:4], vecs[4:5], vecs[5:6]

    for c in copies:
        c.wait()
    wd = wd.ready()

    half_scale, half_shift = 0.5 * scale, 0.5 * shift

    def decode(p, own_rows):
        parts = []
        m = cm[...] * valid_lanes(2 * p)
        for i in range(2):
            t2 = lat[2 * p + i].astype(F32) * half_scale + half_shift
            th = jnp.tanh(t2)
            ts = t2 * th + t2
            parts.append(ts.astype(BF16) * m)
            if own_rows:
                th, t2 = th[h : h + cols], t2[h : h + cols]
                sl = (0.5 + 0.5 * th) * (1.0 + t2 * (1.0 - th))
                sact[2 * p + i - h] = (sl * gain).astype(BF16)
        tt[p, :, 0:width] = nt(wd[...], jnp.concatenate(parts, axis=1))

    def decode_two(p, own_rows):
        decode(p, own_rows)
        decode(p + 1, own_rows)

    loop(0, 4, lambda i: decode_two(2 * i, False))
    loop(4, 12, lambda i: decode_two(2 * i, True))
    loop(12, 16, lambda i: decode_two(2 * i, False))
    o_sact.send()
    w1, w2, w3, w4 = w1.ready(), w2.ready(), w3.ready(), w4.ready()

    pscale = color_column([0.5 / s for s in PIX_STD])
    pbias = color_column([((dbias[k] + 1.0) * 0.5 - PIX_MEAN[k]) * (1.0 / PIX_STD[k]) for k in range(3)])

    def pixels(p):
        c = tt[p, 0:24] + tt[p + 1, 24:48] + tt[p - 1, 48:72]
        x = (lane_taps(c) * pscale + pbias) * (lmask * valid_rows(2 * p))
        z = jnp.zeros((8, 256), F32)
        pixcol[p] = jnp.concatenate([pltpu.roll(x, 1, 1), x, pltpu.roll(x, 255, 1), z], axis=0).astype(BF16)

    def pixels_three(i):
        for k in range(3):
            pixels(1 + 3 * i + k)

    loop(0, (pairs - 2) // 3, pixels_three)

    def first_product(g, buf):
        for i in range(2):
            p = 1 + 2 * g + i
            lhs = pixcol[pl.ds(p - 1, 3), :, 0:width].reshape(96, width)
            buf[8 + i * width : 8 + (i + 1) * width, 0:128] = tn(lhs, w1[...])

    def first_use(g, buf):
        for i in range(2):
            p = 1 + 2 * g + i
            gl, sl = gelu_both(buf[8 + i * width : 8 + (i + 1) * width, 0:128] + b1)
            m = cm[...] * valid_lanes(2 * p)
            f = gl.astype(BF16) * m
            y1[p] = f
            y1n[p - 1, :, 0:64] = f[:, 0:64]
            y1n[p + 1, :, 64:128] = f[:, 64:128]
            slope1[p] = sl.astype(BF16) * m

    pipelined((pairs - 2) // 2, first_product, first_use, (pa, pb))
    o_slope1.send()

    pr = iota((half, width), 0)
    pc = iota((half, width), 1) // 2
    pool[...] = jnp.where(pr == pc, 0.25, 0.0).astype(BF16)

    def second_product(g, buf):
        store_product(buf, both_halves(y1, y1n, 2 + 4 * g, 4), w2[...])

    def second_use(g, buf):
        p0 = 2 + 4 * g
        for i in range(4):
            p = p0 + i
            f, sl = gelu_both(taps(buf, i * width, width, 128) + b2)
            m = cm[...] * valid_lanes(2 * p)
            fi = f.astype(BF16) * m
            feat2[p] = fi
            slope2[p] = sl.astype(BF16) * m
            half_sum = jnp.dot(pool[...], fi, preferred_element_type=F32)
            v = (half_sum + pltpu.roll(half_sum, 64, 1)).astype(BF16)
            k = 1 + 2 * g + i // 2
            if i % 2 == 0:
                yp[k, :, 0:64] = v[:, 0:64]
                ypn[k - 1, :, 0:64] = v[:, 0:64]
            else:
                yp[k, :, 64:128] = v[:, 64:128]
                ypn[k + 1, :, 64:128] = v[:, 64:128]

    pipelined(7, second_product, second_use, (pa, pb))
    o_feat2.send()
    o_slope2.send()

    def third_product(g, buf):
        store_product(buf, both_halves(yp, ypn, 1 + 2 * g, 2), w3[...])

    def wide_use(k0, buf, n, bias, keep):
        for i in range(n):
            m = hm[...] * valid_lanes(4 * (k0 + i))
            for q in range(2):
                f, sl = gelu_both(taps(buf, i * half, half, 256, q * 128, 128) + bias)
                keep(2 * (k0 + i) + q, f.astype(BF16) * m, sl.astype(BF16) * m)

    def third_keep(r, f, sl):
        f3[r] = f
        slope3[r] = sl

    pipelined(7, third_product, lambda g, buf: wide_use(1 + 2 * g, buf, 2, b3, third_keep), (pa, pb))
    o_slope3.send()

    def fourth_product(g, buf):
        lhs = []
        for i in range(4):
            r = 2 * (2 + 4 * g + i)
            lhs.append(jnp.concatenate([f3[r - 1], f3[r], f3[r + 1], f3[r + 2]], axis=1))
        store_product(buf, jnp.concatenate(lhs, axis=0), w4[...])

    def fourth_keep(r, f, sl):
        feat4[r] = f
        slope4[r] = sl
        fm[r] = f * om[...]

    pipelined(3, fourth_product, lambda g, buf: wide_use(2 + 4 * g, buf, 4, b4, fourth_keep), (pa, pb))
    o_feat4.send()
    o_slope4.send()

    a = fm[8:24].reshape(16 * half, 128)
    gram[0:128] = tn(a, a)
    b = feat2[8:24, h : h + cols, :].reshape(16 * cols, 128)
    gram[128:256] = tn(b, b)


def backward_kernel(
    dims,
    idx,
    totals,
    exlow,
    exhigh,
    slope1,
    feat2,
    slope2,
    slope3,
    feat4,
    slope4,
    sact,
    lat,
    norm,
    w4t,
    w3t,
    w2t,
    w1t,
    wdt,
    o_dxh,
    sums,
    loss,
    sw1,
    sw2,
    b4,
    b3,
    y2,
    y2n,
    spread,
    tt,
    brgb,
    pa,
    pb,
):
    rows, cols, image_rows, image_cols, _ = dims
    h = HALO
    width = cols + 2 * h
    half = width // 2
    npix = image_rows * image_cols
    row0 = idx[0] * rows - h
    col0 = idx[1] * cols - h

    def valid_rows(r):
        return jnp.where((row0 + r >= 0) & (row0 + r < image_rows), 1.0, 0.0).astype(F32)

    lane = iota((8, 256), 1)
    lmask = jnp.where((col0 + lane >= 0) & (col0 + lane < image_cols) & (lane < width), 1.0, 0.0)
    lmask = lmask.astype(F32)

    g1 = totals[128:256]
    g1 = g1 + pltpu.roll(pltpu.roll(g1, 64, 0), 64, 1)
    same = (iota((128, 128), 0) // 64) == (iota((128, 128), 1) // 64)
    gap1 = jnp.where(same, g1 * (1.0 / npix) - exlow[...], 0.0)
    gap2 = totals[0:128] * (4.0 / npix) - exhigh[...]
    value = jnp.sum(gap1 * gap1) * (0.5 / 4096.0) + jnp.sum(gap2 * gap2) * (1.0 / 16384.0)
    loss[...] = jnp.broadcast_to(value, loss.shape)
    for gap, sw in ((gap1, sw1), (gap2, sw2)):
        sym = 2.0 * (gap + gap.T)
        upper = sym.astype(BF16)
        sw[0:128] = upper
        sw[128:256] = (sym - upper.astype(F32)).astype(BF16)

    pa[0:8] = jnp.zeros((8, pa.shape[1]), F32)
    pb[0:8] = jnp.zeros((8, pb.shape[1]), F32)
    zrow = jnp.zeros((half, 128), BF16)
    b4[3] = zrow
    b4[28] = zrow
    tt[6] = jnp.zeros((72, 256), F32)
    tt[25] = jnp.zeros((72, 256), F32)
    tt[:, :, 128:256] = jnp.zeros((tt.shape[0], 72, 128), F32)

    def back4(g):
        r0 = 4 + 4 * g
        x = feat4[pl.ds(r0, 4)].reshape(4 * half, 128)
        y = jnp.dot(jnp.concatenate([x, x], axis=1), sw2[...], preferred_element_type=F32)
        y = y * slope4[pl.ds(r0, 4)].reshape(4 * half, 128).astype(F32)
        b4[pl.ds(r0, 4)] = y.astype(BF16).reshape(4, half, 128)

    feat4, slope4 = feat4.ready(), slope4.ready()
    loop(0, 6, back4)
    slope3, w4t, w3t = slope3.ready(), w4t.ready(), w3t.ready()

    def wide(k0, n, src, w, buf):
        lhs = []
        for i in range(n):
            r = 2 * (k0 + i)
            lhs.append(jnp.concatenate([src[r - 1], src[r], src[r + 1], src[r + 2]], axis=1))
        store_product(buf, jnp.concatenate(lhs, axis=0), w[...])

    def back3(g, buf):
        k0 = 2 + 4 * g
        for i in range(4):
            for q in range(2):
                r = 2 * (k0 + i) + q
                part = taps(buf, i * half, half, 256, q * 128, 128)
                b3[r] = (part * slope3[r].astype(F32)).astype(BF16)

    pipelined(3, lambda g, buf: wide(2 + 4 * g, 4, b4, w4t, buf), back3, (pa, pb))
    feat2, slope2 = feat2.ready(), slope2.ready()

    ur = iota((width, width), 0) // 2
    uc = iota((width, width), 1) % half
    spread[...] = jnp.where(ur == uc, 0.25, 0.0).astype(BF16)
    first_half = iota((width, 128), 1) < 64

    def back2(g, buf):
        k0 = 3 + 2 * g
        for i in range(2):
            gp = taps(buf, i * half, half, 128)
            upper = gp.astype(BF16)
            lower = (gp - upper.astype(F32)).astype(BF16)
            r = jnp.dot(spread[...], jnp.concatenate([upper, lower], axis=0), preferred_element_type=F32)
            rr = pltpu.roll(r, 64, 1)
            for q in range(2):
                p = 2 * (k0 + i) + q
                sp = jnp.where(first_half, r, rr) if q == 0 else jnp.where(first_half, rr, r)
                x = feat2[p]
                gt = jnp.dot(jnp.concatenate([x, x], axis=1), sw1[...], preferred_element_type=F32)
                b = ((sp + gt) * slope2[p].astype(F32)).astype(BF16)
                y2[p] = b
                y2n[p - 1, :, 0:64] = b[:, 0:64]
                y2n[p + 1, :, 64:128] = b[:, 64:128]

    pipelined(5, lambda g, buf: wide(3 + 2 * g, 2, b3, w3t, buf), back2, (pa, pb))
    slope1, w2t, w1t = slope1.ready(), w2t.ready(), w1t.ready()

    def back1_product(g, buf):
        store_product(buf, both_halves(y2, y2n, 7 + 3 * g, 3), w2t[...])

    def back1(g, buf):
        for i in range(3):
            p = 7 + 3 * g + i
            b = (taps(buf, i * width, width, 128) * slope1[p].astype(F32)).astype(BF16)
            tt[p, :, 0:width] = nt(w1t[...], b)

    pipelined(6, back1_product, back1, (pa, pb))

    pscale = color_column([0.5 / s for s in PIX_STD])

    def colors(p):
        c = tt[p, 0:24] + tt[p + 1, 24:48] + tt[p - 1, 48:72]
        x = lane_taps(c) * pscale * (lmask * valid_rows(2 * p))
        parts = [pltpu.roll(x, 256 - h + d, 1)[:, 0:cols] for d in (1, 0, -1)]
        z = jnp.zeros((8, cols), F32)
        brgb[p] = jnp.concatenate(parts + [z], axis=0).astype(BF16)

    def colors_three(i):
        for k in range(3):
            colors(7 + 3 * i + k)

    loop(0, 6, colors_three)

    mean, rstd = norm[0:1], norm[1:2]
    offset = mean * rstd
    sact, lat, wdt = sact.ready(), lat.ready(), wdt.ready()
    dxh = o_dxh.ref

    def last_two(i, carry):
        return last(9 + 2 * i, last(8 + 2 * i, carry))

    def last(p, carry):
        s, q = carry
        y = tn(brgb[pl.ds(p - 1, 3)].reshape(96, cols), wdt[...])
        for i in range(2):
            r = 2 * (p - 8) + i
            d = y[:, i * 128 : (i + 1) * 128] * sact[r].astype(F32)
            xh = lat[r].astype(F32) * rstd - offset
            dxh[r] = d.astype(BF16)
            s = s + jnp.sum(d.reshape(cols // 8, 8, 128), axis=0)
            q = q + jnp.sum((d * xh).reshape(cols // 8, 8, 128), axis=0)
        return s, q

    z = jnp.zeros((8, 128), F32)
    s, q = lax.fori_loop(0, 8, last_two, (z, z))
    o_dxh.send()
    sums[...] = jnp.broadcast_to(group_rows(s, q), sums.shape)


def final_kernel(count, lat, dxh, norm, sums, out_hbm, lbuf, dbuf, obuf, sems):
    rows = obuf.shape[0]
    parts = 4
    size = rows // parts
    arriving, leaving = [], []
    for k in range(parts):
        at = pl.ds(k * size, size)
        arriving.append(pltpu.make_async_copy(lat.at[at], lbuf.at[at], sems.at[k]))
        arriving.append(pltpu.make_async_copy(dxh.at[at], dbuf.at[at], sems.at[parts + k]))
        leaving.append(pltpu.make_async_copy(obuf.at[at], out_hbm.at[at], sems.at[2 * parts + k]))
    for c in arriving:
        c.start()
    mean, rstd = norm[0:1], norm[1:2]
    n1, n2 = group_values(sums[...], count)
    b = rstd * rstd * n2
    c = rstd * n1 - b * mean

    def row(r):
        obuf[r] = (dbuf[r].astype(F32) * rstd - lbuf[r].astype(F32) * b - c).astype(BF16)

    for k in range(parts):
        arriving[2 * k].wait()
        arriving[2 * k + 1].wait()
        loop(k * size // 2, (k + 1) * size // 2, lambda i: (row(2 * i), row(2 * i + 1)))
        leaving[k].start()
    for x in leaving:
        x.wait()


def placed_at(x, space):
    return x if INTERPRET else pltpu.with_memory_space_constraint(x, space)


class Arriving:
    def __init__(self, src, dst, sem):
        self.dst = dst
        self.copy = pltpu.make_async_copy(src, dst, sem)
        self.copy.start()

    def ready(self):
        self.copy.wait()
        return self.dst


class Leaving:
    def __init__(self, src, dst, sem):
        self.ref = src
        self.copy = pltpu.make_async_copy(src, dst, sem)

    def send(self):
        self.copy.start()


def call(kernel, outs, scratch, args, kinds, out_kinds):
    spaces = {"s": pltpu.SMEM, "a": pl.ANY,  "d": pl.ANY, "v": pltpu.VMEM, "m": pltpu.VMEM}
    late_in = [i for i, k in enumerate(kinds) if k == "d"]
    late_out = [i for i, k in enumerate(out_kinds) if k == "d"]
    buffers = [pltpu.VMEM(args[i].shape, args[i].dtype) for i in late_in]
    buffers += [pltpu.VMEM(*outs[i]) for i in late_out]
    sems = [pltpu.SemaphoreType.DMA((len(buffers),))] if buffers else []

    def body(*refs):
        refs = list(refs)
        n_in, n_out = len(args), len(outs)
        ins, results, rest = refs[:n_in], refs[n_in : n_in + n_out], refs[n_in + n_out :]
        own, extra = rest[: len(scratch)], rest[len(scratch) :]
        leaving = []
        for j, i in enumerate(late_in):
            ins[i] = Arriving(ins[i], extra[j], extra[-1].at[j])
        for j, i in enumerate(late_out):
            k = len(late_in) + j
            results[i] = Leaving(extra[k], results[i], extra[-1].at[k])
            leaving.append(results[i])
        kernel(*ins, *results, *own)
        for x in leaving:
            x.copy.wait()

    return pl.pallas_call(
        body,
        out_shape=[jax.ShapeDtypeStruct(s, d) if INTERPRET else pltpu.HBM(s, d) for s, d in outs],
        in_specs=[pl.BlockSpec(memory_space=spaces[k]) for k in kinds],
        out_specs=[pl.BlockSpec(memory_space=spaces[k]) for k in out_kinds],
        scratch_shapes=list(scratch) + buffers + sems,
        compiler_params=pltpu.CompilerParams(vmem_limit_bytes=VMEM_LIMIT),
        interpret=INTERPRET,
    )(*[a if k == "s" else placed_at(a, pltpu.VMEM if k == "m" else pltpu.HBM) for a, k in zip(args, kinds)])


def local(
    latent,
    gain,
    bias,
    decoder_weight,
    decoder_bias,
    first_weight,
    first_bias,
    second_weight,
    second_bias,
    third_weight,
    third_bias,
    fourth_weight,
    fourth_bias,
    exemplar_low,
    exemplar_high,
):
    rows, cols, channels = latent.shape
    nrow, ncol = lax.axis_size("row"), lax.axis_size("col")
    n = nrow * ncol
    both = ("row", "col")
    h = HALO
    width = cols + 2 * h
    half = width // 2
    pairs = (rows + 2 * h) // 2
    image_rows, image_cols = rows * nrow, cols * ncol
    count = image_rows * image_cols * (channels // GROUPS)
    dims = (rows, cols, image_rows, image_cols, count)

    def shifted(x, axis, step):
        size = lax.axis_size(axis)
        return lax.ppermute(x, axis, [(i, i + step) for i in range(size) if 0 <= i + step < size])

    def everyone(x):
        return lax.all_to_all(x, both, 0, 0, tiled=True)

    up = shifted(latent[rows - h :], "row", 1)
    down = shifted(latent[:h], "row", -1)
    (mine,) = call(lambda *r: stats_kernel(n, *r), [((n, 128), F32)], [], [latent], "d", "v")
    stats = everyone(mine)
    right_edge, left_edge = call(
        slab_kernel,
        [((2 * pairs, h, 128), BF16)] * 2,
        [pltpu.SemaphoreType.DMA((6,))],
        [latent, up, down],
        "aaa",
        "aa",
    )
    left = shifted(right_edge, "col", 1)
    right = shifted(left_edge, "col", -1)

    idx = jnp.stack([lax.axis_index("row"), lax.axis_index("col"), jnp.int32(0)]).astype(jnp.int32)
    vecs = jnp.concatenate(
        [
            gain,
            bias,
            first_bias,
            first_bias,
            second_bias,
            second_bias,
            third_bias,
            fourth_bias,
            jnp.zeros((256,), F32),
        ]
    ).reshape(8, 128)
    dec = jnp.pad(jnp.transpose(decoder_weight, (0, 1, 3, 2)), ((0, 0), (0, 0), (0, 1), (0, 0)))
    fst = jnp.pad(first_weight, ((0, 0), (0, 0), (0, 1), (0, 0)))
    wd, w1, w2, w3, w4, w4t, w3t, w2t, w1t, wdt = call(
        weights_kernel,
        [
            ((72, 256), BF16),
            ((96, 128), BF16),
            ((256, 384), BF16),
            ((256, 768), BF16),
            ((512, 768), BF16),
            ((512, 768), BF16),
            ((512, 384), BF16),
            ((256, 384), BF16),
            ((72, 128), BF16),
            ((96, 256), BF16),
        ],
        [],
        [
            dec.reshape(36, 128),
            fst.reshape(36, 64),
            second_weight,
            third_weight,
            fourth_weight,
            *narrow_tables(),
        ],
        "v" * 7,
        "v" * 10,
    )

    states = call(
        lambda *r: forward_kernel(dims, *r),
        [
            ((256, 128), F32),
            ((8, 128), F32),
            ((pairs, width, 128), BF16),
            ((pairs, width, 128), BF16),
            ((pairs, width, 128), BF16),
            ((pairs, half, 128), BF16),
            ((pairs, half, 128), BF16),
            ((pairs, half, 128), BF16),
            ((rows, cols, 128), BF16),
        ],
        [
            pltpu.VMEM((2 * pairs, width, 128), BF16),
            pltpu.VMEM((pairs, 72, 256), F32),
            pltpu.VMEM((pairs, 32, 256), BF16),
            pltpu.VMEM((pairs, width, 128), BF16),
            pltpu.VMEM((pairs, width, 128), BF16),
            pltpu.VMEM((pairs // 2, half, 128), BF16),
            pltpu.VMEM((pairs // 2, half, 128), BF16),
            pltpu.VMEM((half, width), BF16),
            pltpu.VMEM((pairs, half, 128), BF16),
            pltpu.VMEM((pairs, half, 128), BF16),
            pltpu.VMEM((width, 128), BF16),
            pltpu.VMEM((half, 128), BF16),
            pltpu.VMEM((half, 128), BF16),
            pltpu.VMEM((4 * width + 16, 768), F32),
            pltpu.VMEM((4 * width + 16, 768), F32),
            pltpu.SemaphoreType.DMA((5,)),
        ],
        [idx, decoder_bias, latent, up, down, left, right, stats, vecs, wd, w1, w2, w3, w4],
        "ssaaammmv" + "d" * 5,
        "vv" + "d" * 7,
    )
    gram, norm = states[:2]
    mine = everyone(gram).reshape(n, 256 // n, 128).sum(axis=0)
    totals = everyone(jnp.broadcast_to(mine[None], (n, 256 // n, 128)).reshape(256, 128))
    exlow = jnp.tile(exemplar_low, (2, 2))

    dxh, sums, loss = call(
        lambda *r: backward_kernel(dims, *r),
        [((rows, cols, 128), BF16), ((n, 128), F32), ((8, 128), F32)],
        [
            pltpu.VMEM((256, 128), BF16),
            pltpu.VMEM((256, 128), BF16),
            pltpu.VMEM((pairs, half, 128), BF16),
            pltpu.VMEM((pairs, half, 128), BF16),
            pltpu.VMEM((pairs, width, 128), BF16),
            pltpu.VMEM((pairs, width, 128), BF16),
            pltpu.VMEM((width, width), BF16),
            pltpu.VMEM((pairs, 72, 256), F32),
            pltpu.VMEM((pairs, 32, cols), BF16),
            pltpu.VMEM((4 * width + 16, 768), F32),
            pltpu.VMEM((4 * width + 16, 768), F32),
        ],
        [idx, totals, exlow, exemplar_high, *states[2:], latent, norm, w4t, w3t, w2t, w1t, wdt],
        "smvv" + "d" * 8 + "v" + "d" * 5,
        "dvv",
    )
    sums = everyone(sums)

    tile = (rows, cols, channels)
    (out,) = call(
        lambda *r: final_kernel(count, *r),
        [(tile, BF16)],
        [pltpu.VMEM(tile, BF16)] * 3 + [pltpu.SemaphoreType.DMA((12,))],
        [latent, dxh, norm, sums],
        "aavm",
        "a",
    )
    return out, loss[0, 0]


def solution(mesh):
    placed = (P("row", "col", None),) + (P(),) * 14
    return jax.shard_map(
        local, mesh=mesh, in_specs=placed, out_specs=(P("row", "col", None), P()), check_vma=False
    )
```

profile of v0, /device:TPU:1, one launch (start us, length us, event | category | flops | bytes accessed | tf_op | source)
XLA Modules:
  0.0 172.6 jit_solution(12261415005041132601)
XLA Ops:
  0.6 1.3 fusion
  1.9 4.4 %collective-permute-start = (bf16[16,128,128]{2,1,0:T(8,128)(2,1)S(1)}, bf16[16,128,128]{2,1,0:T(8,128)(2,1)S(1)}, u32[]{:S(2)}, u32[]{:S(2)}) collective-permute-start(bf16[16,128,128]{2,1,0:T(8,128)(2,1)S(1)} %get-tuple-element.51), channel_id=1, source_target_pairs={{0,8},{8,16},{16,24},{24,32},{32,40},{40,48},{48,56},{56,64},{64,7... | collective-permute-start | bytes 1572872 | tf_op jit(solution)/shard_map/ppermute | solution.py:763
  6.3 1.3 collective-permute-start.1
  7.6 9.2 %collective-permute-done.refs_1_.refs_3_ = bf16[16,128,128]{2,1,0:T(8,128)(2,1)S(1)} collective-permute-done((bf16[16,128,128]{2,1,0:T(8,128)(2,1)S(1)}, bf16[16,128,128]{2,1,0:T(8,128)(2,1)S(1)}, u32[]{:S(2)}, u32[]{:S(2)}) %collective-permute-start) | collective-permute-done | bytes 524320 | tf_op jit(solution)/shard_map/ppermute | solution.py:763
  16.9 4.2 %collective-permute-done.1.refs_2_.refs_4_ = bf16[16,128,128]{2,1,0:T(8,128)(2,1)S(1)} collective-permute-done((bf16[16,128,128]{2,1,0:T(8,128)(2,1)S(1)}, bf16[16,128,128]{2,1,0:T(8,128)(2,1)S(1)}, u32[]{:S(2)}, u32[]{:S(2)}) %collective-permute-start.1) | collective-permute-done | bytes 524320 | tf_op jit(solution)/shard_map/ppermute | solution.py:763
  21.1 0.8 copy-done.2
  21.9 17.0 %shard_map.176 = (bf16[64,16,128]{2,1,0:T(8,128)(2,1)}, bf16[64,16,128]{2,1,0:T(8,128)(2,1)}) custom-call(bf16[32,128,128]{2,1,0:T(8,128)(2,1)} %refs_0_.5, bf16[16,128,128]{2,1,0:T(8,128)(2,1)} %copy-done.1, bf16[16,128,128]{2,1,0:T(8,128)(2,1)} %copy-done.2), custom_call_target="tpu_custom_call" | custom-call | tf_op jit(solution)/shard_map/pallas_call | solution.py:721
  39.0 4.9 %collective-permute-start.2 = (bf16[64,16,128]{2,1,0:T(8,128)(2,1)}, bf16[64,16,128]{2,1,0:T(8,128)(2,1)S(1)}, u32[]{:S(2)}, u32[]{:S(2)}) collective-permute-start(bf16[64,16,128]{2,1,0:T(8,128)(2,1)} %get-tuple-element.26), channel_id=1, source_target_pairs={{0,1},{1,2},{2,3},{3,4},{4,5},{5,6},{6,7},{8,9},{9,10},{10,11},{11... | collective-permute-start | bytes 786440 | tf_op jit(solution)/shard_map/ppermute | solution.py:763
  43.9 1.9 %collective-permute-start.3 = (bf16[64,16,128]{2,1,0:T(8,128)(2,1)}, bf16[64,16,128]{2,1,0:T(8,128)(2,1)S(1)}, u32[]{:S(2)}, u32[]{:S(2)}) collective-permute-start(bf16[64,16,128]{2,1,0:T(8,128)(2,1)} %get-tuple-element.27), channel_id=1, source_target_pairs={{1,0},{2,1},{3,2},{4,3},{5,4},{6,5},{7,6},{9,8},{10,9},{11,10},{12... | collective-permute-start | bytes 786440 | tf_op jit(solution)/shard_map/ppermute | solution.py:763
  45.8 2.4 %shard_map.177 = f32[256,128]{1,0:T(8,128)} custom-call(bf16[32,128,128]{2,1,0:T(8,128)(2,1)} %refs_0_.5), custom_call_target="tpu_custom_call" | custom-call | tf_op jit(solution)/shard_map/pallas_call | solution.py:721
  48.2 14.4 %all-to-all-start = ((f32[256,1,128]{2,1,0:T(1,128)}), f32[256,1,128]{2,1,0:T(1,128)S(1)}, u32[]{:S(2)}, u32[]{:S(2)}) async-start(f32[256,1,128]{2,1,0:T(1,128)} %bitcast.20), calls=%async_computation | async-start | bytes 262144 | tf_op jit(solution)/shard_map/all_to_all | solution.py:766
  63.9 3.3 %shard_map.178 = (bf16[72,256]{1,0:T(8,128)(2,1)}, bf16[96,128]{1,0:T(8,128)(2,1)}, bf16[256,384]{1,0:T(8,128)(2,1)}, bf16[256,768]{1,0:T(8,128)(2,1)}, bf16[512...) custom-call(bf16[36,128]{1,0:T(8,128)(2,1)} %reshape.35.refs_0_, ...), custom_call_target="tpu_custom_call" | custom-call | tf_op jit(solution)/shard_map/pallas_call | solution.py:721
  68.0 7.5 %all-to-all-done = f32[256,1,128]{2,1,0:T(1,128)S(1)} async-done(((f32[256,1,128]{2,1,0:T(1,128)}), f32[256,1,128]{2,1,0:T(1,128)S(1)}, u32[]{:S(2)}, u32[]{:S(2)}) %all-to-all-start) | async-done | bytes 131104 | tf_op jit(solution)/shard_map/all_to_all | solution.py:766
  75.5 22.6 %shard_map.179 = (f32[256,128]{1,0:T(8,128)}, f32[8,128]{1,0:T(8,128)}, bf16[32,160,128]{2,1,0:T(8,128)(2,1)}, bf16[32,160,128]{2,1,0:T(8,128)(2,1)}, bf16[32,16...) custom-call(s32[3]{0:T(128)S(1)} %pad_add_fusion.refs_0_, ...), custom_call_target="tpu_custom_call" | custom-call | tf_op jit(solution)/shard_map/pallas_call | solution.py:721
  98.0 19.1 %all_to_all.39 = f32[256,1,128]{2,1,0:T(1,128)S(1)} all-to-all(f32[256,1,128]{2,1,0:T(1,128)} %bitcast.22), channel_id=1, replica_groups=mesh['row'=32,'col'=8] {'row','col'}, dimensions={0} | all-to-all | bytes 262144 | tf_op jit(solution)/shard_map/all_to_all | solution.py:766
  117.4 0.7 reshape.37
  118.1 5.5 %all-to-all-start.2 = ((f32[256,1,128]{2,1,0:T(1,128)}), f32[256,1,128]{2,1,0:T(1,128)S(1)}, u32[]{:S(2)}, u32[]{:S(2)}) async-start(f32[256,1,128]{2,1,0:T(1,128)} %reshape.37), calls=%async_computation.2 | async-start | bytes 262144 | tf_op jit(solution)/shard_map/all_to_all | solution.py:766
  123.7 0.7 tile.10.refs_2_
  124.5 12.2 %all-to-all-done.2 = f32[256,1,128]{2,1,0:T(1,128)S(1)} async-done(((f32[256,1,128]{2,1,0:T(1,128)}), f32[256,1,128]{2,1,0:T(1,128)S(1)}, u32[]{:S(2)}, u32[]{:S(2)}) %all-to-all-start.2) | async-done | bytes 131104 | tf_op jit(solution)/shard_map/all_to_all | solution.py:766
  136.7 14.2 %shard_map.180 = (bf16[32,128,128]{2,1,0:T(8,128)(2,1)}, f32[256,128]{1,0:T(8,128)}, f32[8,128]{1,0:T(8,128)}) custom-call(s32[3]{0:T(128)S(1)} %pad_add_fusion.refs_0_, f32[256,128]{1,0:T(8,128)S(1)} %bitcast.17, f32[128,128]{1,0:T(8,128)} %tile.10.refs_2_, f32[128,128]{1,0:T(8,128)} %refs_3_.3, bf16[32,160,128]{2,1,0:T(8,128)(2,1)} %get-tuple-element.34.refs_4_, ...), custom_call_target="tpu_custom_call" | custom-call | tf_op jit(solution)/shard_map/pallas_call | solution.py:721
  150.8 5.4 %all-to-all-start.3 = ((f32[256,1,128]{2,1,0:T(1,128)}), f32[256,1,128]{2,1,0:T(1,128)S(1)}, u32[]{:S(2)}, u32[]{:S(2)}) async-start(f32[256,1,128]{2,1,0:T(1,128)} %bitcast.21), calls=%async_computation.3 | async-start | bytes 262144 | tf_op jit(solution)/shard_map/all_to_all | solution.py:766
  156.3 1.2 slice.11
  157.5 11.8 %all-to-all-done.3 = f32[256,1,128]{2,1,0:T(1,128)S(1)} async-done(((f32[256,1,128]{2,1,0:T(1,128)}), f32[256,1,128]{2,1,0:T(1,128)S(1)}, u32[]{:S(2)}, u32[]{:S(2)}) %all-to-all-start.3) | async-done | bytes 131104 | tf_op jit(solution)/shard_map/all_to_all | solution.py:766
  169.3 3.1 %shard_map.181 = bf16[32,128,128]{2,1,0:T(8,128)(2,1)} custom-call(bf16[32,128,128]{2,1,0:T(8,128)(2,1)} %refs_0_.5, bf16[32,128,128]{2,1,0:T(8,128)(2,1)} %get-tuple-element.47.refs_1_, f32[8,128]{1,0:T(8,128)} %get-tuple-element.41.refs_12_.refs_2_, f32[256,128]{1,0:T(8,128)S(1)} %bitcast.19), custom_call_target="tpu_custom_call" | custom-call | tf_op jit(solution)/shard_map/pallas_call | solution.py:721
  (34 shorter events, 2.4 us)
Async XLA Ops:
  1.9 15.0 %collective-permute-start = (bf16[16,128,128]{2,1,0:T(8,128)(2,1)S(1)}, bf16[16,128,128]{2,1,0:T(8,128)(2,1)S(1)}, u32[]{:S(2)}, u32[]{:S(2)}) collective-permute-start(bf16[16,128,128]{2,1,0:T(8,128)(2,1)S(1)} %get-tuple-element.51), channel_id=1, source_target_pairs={{0,8},{8,16},{16,24},{24,32},{32,40},{40,48},{48,56},{56,64},{64,7... | collective-permute-start | bytes 1572872 | tf_op jit(solution)/shard_map/ppermute | solution.py:763
  6.3 56.3 %copy-start.4 = (bf16[3,3,128,3]{2,3,1,0:T(4,128)(2,1)S(1)}, bf16[3,3,128,3]{2,3,1,0:T(4,128)(2,1)}, u32[]{:S(2)}) copy-start(bf16[3,3,128,3]{2,3,1,0:T(4,128)(2,1)} %param.20) | copy-start | bytes 20740
  6.3 56.9 %copy-start.5 = (bf16[3,3,3,64]{3,2,1,0:T(4,128)(2,1)S(1)}, bf16[3,3,3,64]{3,2,1,0:T(4,128)(2,1)}, u32[]{:S(2)}) copy-start(bf16[3,3,3,64]{3,2,1,0:T(4,128)(2,1)} %param.22) | copy-start | bytes 10372
  6.3 14.7 %collective-permute-start.1 = (bf16[16,128,128]{2,1,0:T(8,128)(2,1)S(1)}, bf16[16,128,128]{2,1,0:T(8,128)(2,1)S(1)}, u32[]{:S(2)}, u32[]{:S(2)}) collective-permute-start(bf16[16,128,128]{2,1,0:T(8,128)(2,1)S(1)} %get-tuple-element.50), channel_id=1, source_target_pairs={{8,0},{16,8},{24,16},{32,24},{40,32},{48,40},{56,48},{64,56},{72,6... | collective-permute-start | bytes 1572872 | tf_op jit(solution)/shard_map/ppermute | solution.py:763
  16.9 4.2 %copy-start.1 = (bf16[16,128,128]{2,1,0:T(8,128)(2,1)}, bf16[16,128,128]{2,1,0:T(8,128)(2,1)S(1)}, u32[]{:S(2)}) copy-start(bf16[16,128,128]{2,1,0:T(8,128)(2,1)S(1)} %collective-permute-done.refs_1_.refs_3_) | copy-start | bytes 1572868
  21.1 0.8 copy-start.2
  38.9 28.2 %copy-start.6 = (f32[64]{0:T(128)S(1)}, f32[64]{0:T(128)}, u32[]{:S(2)}) copy-start(f32[64]{0:T(128)} %param.23) | copy-start | bytes 772
  38.9 28.2 %copy-start.7 = (f32[64]{0:T(128)S(1)}, f32[64]{0:T(128)}, u32[]{:S(2)}) copy-start(f32[64]{0:T(128)} %param.25) | copy-start | bytes 772
  38.9 28.2 %copy-start.8 = (f32[128]{0:T(128)S(1)}, f32[128]{0:T(128)}, u32[]{:S(2)}) copy-start(f32[128]{0:T(128)} %param.18) | copy-start | bytes 1540
  39.0 28.2 %copy-start.9 = (f32[128]{0:T(128)S(1)}, f32[128]{0:T(128)}, u32[]{:S(2)}) copy-start(f32[128]{0:T(128)} %param.19) | copy-start | bytes 1540
  39.0 28.2 %copy-start.10 = (f32[128]{0:T(128)S(1)}, f32[128]{0:T(128)}, u32[]{:S(2)}) copy-start(f32[128]{0:T(128)} %param.27) | copy-start | bytes 1540
  39.0 28.2 %copy-start.11 = (f32[128]{0:T(128)S(1)}, f32[128]{0:T(128)}, u32[]{:S(2)}) copy-start(f32[128]{0:T(128)} %param.29) | copy-start | bytes 1540
  39.0 36.5 %copy-start = (f32[3]{0:T(128)S(1)}, f32[3]{0:T(128)}, u32[]{:S(2)}) copy-start(f32[3]{0:T(128)} %refs_1_.1) | copy-start | bytes 40
  39.0 36.4 %collective-permute-start.2 = (bf16[64,16,128]{2,1,0:T(8,128)(2,1)}, bf16[64,16,128]{2,1,0:T(8,128)(2,1)S(1)}, u32[]{:S(2)}, u32[]{:S(2)}) collective-permute-start(bf16[64,16,128]{2,1,0:T(8,128)(2,1)} %get-tuple-element.26), channel_id=1, source_target_pairs={{0,1},{1,2},{2,3},{3,4},{4,5},{5,6},{6,7},{8,9},{9,10},{10,11},{11... | collective-permute-start | bytes 786440 | tf_op jit(solution)/shard_map/ppermute | solution.py:763
  43.9 31.6 %collective-permute-start.3 = (bf16[64,16,128]{2,1,0:T(8,128)(2,1)}, bf16[64,16,128]{2,1,0:T(8,128)(2,1)S(1)}, u32[]{:S(2)}, u32[]{:S(2)}) collective-permute-start(bf16[64,16,128]{2,1,0:T(8,128)(2,1)} %get-tuple-element.27), channel_id=1, source_target_pairs={{1,0},{2,1},{3,2},{4,3},{5,4},{6,5},{7,6},{9,8},{10,9},{11,10},{12... | collective-permute-start | bytes 786440 | tf_op jit(solution)/shard_map/ppermute | solution.py:763
  48.2 27.3 %all-to-all-start = ((f32[256,1,128]{2,1,0:T(1,128)}), f32[256,1,128]{2,1,0:T(1,128)S(1)}, u32[]{:S(2)}, u32[]{:S(2)}) async-start(f32[256,1,128]{2,1,0:T(1,128)} %bitcast.20), calls=%async_computation | async-start | bytes 262144 | tf_op jit(solution)/shard_map/all_to_all | solution.py:766
  75.5 48.2 %copy-start.3 = (f32[64,64]{1,0:T(8,128)S(1)}, f32[64,64]{1,0:T(8,128)}, u32[]{:S(2)}) copy-start(f32[64,64]{1,0:T(8,128)} %param.30) | copy-start | bytes 49156
  118.1 18.5 %all-to-all-start.2 = ((f32[256,1,128]{2,1,0:T(1,128)}), f32[256,1,128]{2,1,0:T(1,128)S(1)}, u32[]{:S(2)}, u32[]{:S(2)}) async-start(f32[256,1,128]{2,1,0:T(1,128)} %reshape.37), calls=%async_computation.2 | async-start | bytes 262144 | tf_op jit(solution)/shard_map/all_to_all | solution.py:766
  150.8 18.4 %all-to-all-start.3 = ((f32[256,1,128]{2,1,0:T(1,128)}), f32[256,1,128]{2,1,0:T(1,128)S(1)}, u32[]{:S(2)}, u32[]{:S(2)}) async-start(f32[256,1,128]{2,1,0:T(1,128)} %bitcast.21), calls=%async_computation.3 | async-start | bytes 262144 | tf_op jit(solution)/shard_map/all_to_all | solution.py:766
where the time goes:
time: 173 us
  Pallas kernels  62.6 us (36%)
  waiting for transfers between devices  44.9 us (26%)
  starting transfers between devices  37.8 us (22%)
  blocking collectives  19.1 us (11%)
  local copies, waits for them, and re-layouts  6.75 us (4%)
    pallas_call x6, Pallas kernels, call(): pl.pallas_call(body, out_shape=[jax.ShapeDtypeStruct(s, d) if INTERPRET e...  62.6 us
    all_to_all x3, waiting for transfers between devices, everyone(): return lax.all_to_all(x, both, 0, 0, tiled=True)  31.5 us
    all_to_all x3, starting transfers between devices, everyone(): return lax.all_to_all(x, both, 0, 0, tiled=True)  25.4 us
    all_to_all x1, blocking collectives, everyone(): return lax.all_to_all(x, both, 0, 0, tiled=True)  19.1 us
    ppermute x4, waiting for transfers between devices, shifted(): lax.ppermute(x, axis, [(i, i + step) for i in range(size) if 0 <= i + ste...  13.4 us
    ppermute x4, starting transfers between devices, shifted(): lax.ppermute(x, axis, [(i, i + step) for i in range(size) if 0 <= i + ste...  12.5 us
  transfers between devices with their start and end apart: 7, of which 5 were waited for; matrix products, arithmetic and copies ran while one was open for 2% of the time, Pallas kernels for 3%

commit v1 on v0

--- a/solution.py
+++ b/solution.py
@@ -46,38 +46,49 @@
     return jnp.asarray(outs, BF16), jnp.asarray(ins, BF16)
 
 
-def weights_kernel(dec, fst, w2r, w3r, w4r, outs, ins, wd, w1, w2, w3, w4, w4t, w3t, w2t, w1t, wdt):
+def place(t, x):
+    return jnp.dot(t, x, preferred_element_type=F32)
+
+
+def tap(w, dy, dx):
+    return w[dy, dx] if 0 <= dy < 3 else jnp.zeros(w.shape[2:], BF16)
+
+
+def forward_weights(dec, fst, w2r, w3r, w4r, outs, ins, wd, w1, w2, w3, w4):
     d, f = dec[...], fst[...]
-
-    def place(t, x):
-        return jnp.dot(t, x, preferred_element_type=F32)
-
     for i in range(2):
         wd[:, i * 128 : (i + 1) * 128] = place(outs[i], d).astype(BF16)
-        wdt[:, i * 128 : (i + 1) * 128] = place(ins[2 + i], d).astype(BF16)
     w1[...] = jnp.concatenate([place(ins[0], f), place(ins[1], f)], axis=1).astype(BF16)
-    w1t[...] = jnp.concatenate([place(outs[2], f), place(outs[3], f)], axis=1).astype(BF16)
-
-    def tap(w, dy, dx, rows, cols):
-        return w[dy, dx] if 0 <= dy < 3 else jnp.zeros((rows, cols), BF16)
-
     for k, j in enumerate((1, 2, 3, 0)):
         for dx in range(3):
-            pair = [tap(w2r, j - q, dx, 64, 64) for q in range(2)]
+            pair = [tap(w2r, j - q, dx) for q in range(2)]
             w2[k * 64 : (k + 1) * 64, dx * 128 : (dx + 1) * 128] = jnp.concatenate(pair, axis=1)
-            pair = [tap(w2r, 2 - j + q, 2 - dx, 64, 64) for q in range(2)]
-            w2t[k * 64 : (k + 1) * 64, dx * 128 : (dx + 1) * 128] = jnp.concatenate(pair, axis=0).T
             for q in range(2):
                 at = dx * 256 + q * 128
-                w3[k * 64 : (k + 1) * 64, at : at + 128] = tap(w3r, j - q, dx, 64, 128)
+                w3[k * 64 : (k + 1) * 64, at : at + 128] = tap(w3r, j - q, dx)
     for j in range(4):
         for dx in range(3):
-            pair = [tap(w3r, 2 - j + q, 2 - dx, 64, 128) for q in range(2)]
+            for q in range(2):
+                at = dx * 256 + q * 128
+                w4[j * 128 : (j + 1) * 128, at : at + 128] = tap(w4r, j - q, dx)
+
+
+def backward_weights(dec, fst, w2r, w3r, w4r, outs, ins, w4t, w3t, w2t, w1t, wdt):
+    d, f = dec[...], fst[...]
+    for i in range(2):
+        wdt[:, i * 128 : (i + 1) * 128] = place(ins[2 + i], d).astype(BF16)
+    w1t[...] = jnp.concatenate([place(outs[2], f), place(outs[3], f)], axis=1).astype(BF16)
+    for k, j in enumerate((1, 2, 3, 0)):
+        for dx in range(3):
+            pair = [tap(w2r, 2 - j + q, 2 - dx) for q in range(2)]
+            w2t[k * 64 : (k + 1) * 64, dx * 128 : (dx + 1) * 128] = jnp.concatenate(pair, axis=0).T
+    for j in range(4):
+        for dx in range(3):
+            pair = [tap(w3r, 2 - j + q, 2 - dx) for q in range(2)]
             w3t[j * 128 : (j + 1) * 128, dx * 128 : (dx + 1) * 128] = jnp.concatenate(pair, axis=0).T
             for q in range(2):
                 at = dx * 256 + q * 128
-                w4[j * 128 : (j + 1) * 128, at : at + 128] = tap(w4r, j - q, dx, 128, 128)
-                w4t[j * 128 : (j + 1) * 128, at : at + 128] = tap(w4r, 2 - j + q, 2 - dx, 128, 128).T
+                w4t[j * 128 : (j + 1) * 128, at : at + 128] = tap(w4r, 2 - j + q, 2 - dx).T
 
 
 def iota(shape, axis):
@@ -217,18 +228,12 @@
     o_ref[...] = jnp.broadcast_to(group_rows(s, q), (n, 128))
 
 
-def slab_kernel(x, up, down, right, left, sems):
+def slab_kernel(x, up, down, right, left):
     rows, cols, _ = x.shape
     h = HALO
-    copies = []
     for out, at in ((right, cols - h), (left, 0)):
         for src, r in ((up, 0), (x, h), (down, h + rows)):
-            k = len(copies)
-            dst = out.at[pl.ds(r, src.shape[0])]
-            copies.append(pltpu.make_async_copy(src.at[:, pl.ds(at, h)], dst, sems.at[k]))
-            copies[-1].start()
-    for c in copies:
-        c.wait()
+            out[r : r + src.shape[0]] = src[:, at : at + h]
 
 
 def forward_kernel(
@@ -675,8 +680,8 @@
 
 
 class Arriving:
-    def __init__(self, src, dst, sem):
-        self.dst = dst
+    def __init__(self, src, dst, sem, whole):
+        self.dst = whole
         self.copy = pltpu.make_async_copy(src, dst, sem)
         self.copy.start()
 
@@ -686,15 +691,15 @@
 
 
 class Leaving:
-    def __init__(self, src, dst, sem):
-        self.ref = src
+    def __init__(self, src, dst, sem, whole):
+        self.ref = whole
         self.copy = pltpu.make_async_copy(src, dst, sem)
 
     def send(self):
         self.copy.start()
 
 
-def call(kernel, outs, scratch, args, kinds, out_kinds):
+def call(kernel, outs, scratch, args, kinds, out_kinds, order=None, spans=None, out_spans=None):
     spaces = {"s": pltpu.SMEM, "a": pl.ANY,  "d": pl.ANY, "v": pltpu.VMEM, "m": pltpu.VMEM}
     late_in = [i for i, k in enumerate(kinds) if k == "d"]
     late_out = [i for i, k in enumerate(out_kinds) if k == "d"]
@@ -708,11 +713,14 @@
         ins, results, rest = refs[:n_in], refs[n_in : n_in + n_out], refs[n_in + n_out :]
         own, extra = rest[: len(scratch)], rest[len(scratch) :]
         leaving = []
-        for j, i in enumerate(late_in):
-            ins[i] = Arriving(ins[i], extra[j], extra[-1].at[j])
+        for i in order or late_in:
+            j = late_in.index(i)
+            at = (spans or {}).get(i, slice(None))
+            ins[i] = Arriving(ins[i].at[at], extra[j].at[at], extra[-1].at[j], extra[j])
         for j, i in enumerate(late_out):
             k = len(late_in) + j
-            results[i] = Leaving(extra[k], results[i], extra[-1].at[k])
+            at = (out_spans or {}).get(i, slice(None))
+            results[i] = Leaving(extra[k].at[at], results[i].at[at], extra[-1].at[k], extra[k])
             leaving.append(results[i])
         kernel(*ins, *results, *own)
         for x in leaving:
@@ -772,10 +780,10 @@
     right_edge, left_edge = call(
         slab_kernel,
         [((2 * pairs, h, 128), BF16)] * 2,
-        [pltpu.SemaphoreType.DMA((6,))],
+        [],
         [latent, up, down],
-        "aaa",
-        "aa",
+        "vvv",
+        "vv",
     )
     left = shifted(right_edge, "col", 1)
     right = shifted(left_edge, "col", -1)
@@ -796,32 +804,18 @@
     ).reshape(8, 128)
     dec = jnp.pad(jnp.transpose(decoder_weight, (0, 1, 3, 2)), ((0, 0), (0, 0), (0, 1), (0, 0)))
     fst = jnp.pad(first_weight, ((0, 0), (0, 0), (0, 1), (0, 0)))
-    wd, w1, w2, w3, w4, w4t, w3t, w2t, w1t, wdt = call(
-        weights_kernel,
-        [
-            ((72, 256), BF16),
-            ((96, 128), BF16),
-            ((256, 384), BF16),
-            ((256, 768), BF16),
-            ((512, 768), BF16),
-            ((512, 768), BF16),
-            ((512, 384), BF16),
-            ((256, 384), BF16),
-            ((72, 128), BF16),
-            ((96, 256), BF16),
-        ],
-        [],
-        [
-            dec.reshape(36, 128),
-            fst.reshape(36, 64),
-            second_weight,
-            third_weight,
-            fourth_weight,
-            *narrow_tables(),
-        ],
-        "v" * 7,
-        "v" * 10,
-    )
+    sources = [
+        dec.reshape(36, 128),
+        fst.reshape(36, 64),
+        second_weight,
+        third_weight,
+        fourth_weight,
+        *narrow_tables(),
+    ]
+    shapes = ((72, 256), (96, 128), (256, 384), (256, 768), (512, 768))
+    ahead = call(forward_weights, [(x, BF16) for x in shapes], [], sources, "v" * 7, "v" * 5)
+    shapes = ((512, 768), (512, 384), (256, 384), (72, 128), (96, 256))
+    back = call(backward_weights, [(x, BF16) for x in shapes], [], sources, "v" * 7, "v" * 5)
 
     states = call(
         lambda *r: forward_kernel(dims, *r),
@@ -854,9 +848,17 @@
             pltpu.VMEM((4 * width + 16, 768), F32),
             pltpu.SemaphoreType.DMA((5,)),
         ],
-        [idx, decoder_bias, latent, up, down, left, right, stats, vecs, wd, w1, w2, w3, w4],
+        [idx, decoder_bias, latent, up, down, left, right, stats, vecs, *ahead],
         "ssaaammmv" + "d" * 5,
         "vv" + "d" * 7,
+        out_spans={
+            2: slice(7, 25),
+            3: slice(6, 26),
+            4: slice(6, 26),
+            5: slice(4, 28),
+            6: slice(4, 28),
+            7: slice(4, 28),
+        },
     )
     gram, norm = states[:2]
     mine = everyone(gram).reshape(n, 256 // n, 128).sum(axis=0)
@@ -879,9 +881,11 @@
             pltpu.VMEM((4 * width + 16, 768), F32),
             pltpu.VMEM((4 * width + 16, 768), F32),
         ],
-        [idx, totals, exlow, exemplar_high, *states[2:], latent, norm, w4t, w3t, w2t, w1t, wdt],
+        [idx, totals, exlow, exemplar_high, *states[2:], latent, norm, *back],
         "smvv" + "d" * 8 + "v" + "d" * 5,
         "dvv",
+        order=(8, 9, 13, 7, 14, 5, 6, 15, 4, 16, 10, 11, 17),
+        spans={4: slice(7, 25), 5: slice(6, 26), 6: slice(6, 26), 7: slice(4, 28), 8: slice(4, 28), 9: slice(4, 28)},
     )
     sums = everyone(sums)
 

time: 173 us -> 157 us (0.908)
  Pallas kernels: 62.6 us -> 48.2 us
  waiting for transfers between devices: 44.9 us -> 42.8 us
    pallas_call x6 -> x7, Pallas kernels: 62.6 us -> 48.2 us  [call(): pl.pallas_call(body, out_shape=[jax.ShapeDtypeStruct(s, d) if INTERPRET e...]
    all_to_all x3, waiting for transfers between devices: 31.5 us -> 29.3 us  [everyone(): return lax.all_to_all(x, both, 0, 0, tiled=True)]
  transfers between devices with their start and end apart: 7 -> 7, of which waited for: 5 -> 5; matrix products, arithmetic and copies ran while one was open for 2% -> 3% of each run, Pallas kernels for 3% -> 5%
where the time goes in v1:
time: 157 us; the launch traced here: 156 us
  Pallas kernels  48.2 us (31%)
  waiting for transfers between devices  42.8 us (27%)
  starting transfers between devices  37.9 us (24%)
  blocking collectives  19.1 us (12%)
  local copies, waits for them, and re-layouts  6.71 us (4%)
    pallas_call x7, Pallas kernels, call(): pl.pallas_call(body, out_shape=[jax.ShapeDtypeStruct(s, d) if INTERPRET e...  48.2 us
    all_to_all x3, waiting for transfers between devices, everyone(): return lax.all_to_all(x, both, 0, 0, tiled=True)  29.3 us
    all_to_all x3, starting transfers between devices, everyone(): return lax.all_to_all(x, both, 0, 0, tiled=True)  25.4 us
    all_to_all x1, blocking collectives, everyone(): return lax.all_to_all(x, both, 0, 0, tiled=True)  19.1 us
    ppermute x4, waiting for transfers between devices, shifted(): lax.ppermute(x, axis, [(i, i + step) for i in range(size) if 0 <= i + ste...  13.4 us
    ppermute x4, starting transfers between devices, shifted(): lax.ppermute(x, axis, [(i, i + step) for i in range(size) if 0 <= i + ste...  12.5 us
  transfers between devices with their start and end apart: 7, of which 5 were waited for; matrix products, arithmetic and copies ran while one was open for 3% of the time, Pallas kernels for 5%

profile of v1, /device:TPU:1, one launch (start us, length us, event | category | flops | bytes accessed | tf_op | source)
XLA Modules:
  0.0 156.1 jit_solution(8873854213316059979)
XLA Ops:
  0.6 1.3 fusion
  1.9 4.4 %collective-permute-start = (bf16[16,128,128]{2,1,0:T(8,128)(2,1)S(1)}, bf16[16,128,128]{2,1,0:T(8,128)(2,1)S(1)}, u32[]{:S(2)}, u32[]{:S(2)}) collective-permute-start(bf16[16,128,128]{2,1,0:T(8,128)(2,1)S(1)} %get-tuple-element.51), channel_id=1, source_target_pairs={{0,8},{8,16},{16,24},{24,32},{32,40},{40,48},{48,56},{56,64},{64,7... | collective-permute-start | bytes 1572872 | tf_op jit(solution)/shard_map/ppermute | solution.py:771
  6.3 1.3 collective-permute-start.1
  7.6 9.2 %collective-permute-done.refs_1_.refs_3_ = bf16[16,128,128]{2,1,0:T(8,128)(2,1)S(1)} collective-permute-done((bf16[16,128,128]{2,1,0:T(8,128)(2,1)S(1)}, bf16[16,128,128]{2,1,0:T(8,128)(2,1)S(1)}, u32[]{:S(2)}, u32[]{:S(2)}) %collective-permute-start) | collective-permute-done | bytes 524320 | tf_op jit(solution)/shard_map/ppermute | solution.py:771
  16.9 4.2 %collective-permute-done.1.refs_2_.refs_4_ = bf16[16,128,128]{2,1,0:T(8,128)(2,1)S(1)} collective-permute-done((bf16[16,128,128]{2,1,0:T(8,128)(2,1)S(1)}, bf16[16,128,128]{2,1,0:T(8,128)(2,1)S(1)}, u32[]{:S(2)}, u32[]{:S(2)}) %collective-permute-start.1) | collective-permute-done | bytes 524320 | tf_op jit(solution)/shard_map/ppermute | solution.py:771
  21.1 0.8 copy-done.2
  21.9 2.3 %shard_map.176 = (bf16[64,16,128]{2,1,0:T(8,128)(2,1)}, bf16[64,16,128]{2,1,0:T(8,128)(2,1)}) custom-call(bf16[32,128,128]{2,1,0:T(8,128)(2,1)} %refs_0_.5, bf16[16,128,128]{2,1,0:T(8,128)(2,1)} %copy-done.1, bf16[16,128,128]{2,1,0:T(8,128)(2,1)} %copy-done.2), custom_call_target="tpu_custom_call" | custom-call | tf_op jit(solution)/shard_map/pallas_call | solution.py:729
  24.2 4.9 %collective-permute-start.2 = (bf16[64,16,128]{2,1,0:T(8,128)(2,1)}, bf16[64,16,128]{2,1,0:T(8,128)(2,1)S(1)}, u32[]{:S(2)}, u32[]{:S(2)}) collective-permute-start(bf16[64,16,128]{2,1,0:T(8,128)(2,1)} %get-tuple-element.26), channel_id=1, source_target_pairs={{0,1},{1,2},{2,3},{3,4},{4,5},{5,6},{6,7},{8,9},{9,10},{10,11},{11... | collective-permute-start | bytes 786440 | tf_op jit(solution)/shard_map/ppermute | solution.py:771
  29.1 1.9 %collective-permute-start.3 = (bf16[64,16,128]{2,1,0:T(8,128)(2,1)}, bf16[64,16,128]{2,1,0:T(8,128)(2,1)S(1)}, u32[]{:S(2)}, u32[]{:S(2)}) collective-permute-start(bf16[64,16,128]{2,1,0:T(8,128)(2,1)} %get-tuple-element.27), channel_id=1, source_target_pairs={{1,0},{2,1},{3,2},{4,3},{5,4},{6,5},{7,6},{9,8},{10,9},{11,10},{12... | collective-permute-start | bytes 786440 | tf_op jit(solution)/shard_map/ppermute | solution.py:771
  31.1 2.4 %shard_map.177 = f32[256,128]{1,0:T(8,128)} custom-call(bf16[32,128,128]{2,1,0:T(8,128)(2,1)} %refs_0_.5), custom_call_target="tpu_custom_call" | custom-call | tf_op jit(solution)/shard_map/pallas_call | solution.py:729
  33.4 14.4 %all-to-all-start = ((f32[256,1,128]{2,1,0:T(1,128)}), f32[256,1,128]{2,1,0:T(1,128)S(1)}, u32[]{:S(2)}, u32[]{:S(2)}) async-start(f32[256,1,128]{2,1,0:T(1,128)} %bitcast.20), calls=%async_computation | async-start | bytes 262144 | tf_op jit(solution)/shard_map/all_to_all | solution.py:774
  49.1 2.6 %shard_map.178 = (bf16[72,256]{1,0:T(8,128)(2,1)}, bf16[96,128]{1,0:T(8,128)(2,1)}, bf16[256,384]{1,0:T(8,128)(2,1)}, bf16[256,768]{1,0:T(8,128)(2,1)}, bf16[512,768]{1,0:T(8,128)(2,1)}) custom-call(bf16[36,128]{1,0:T(8,128)(2,1)} %reshape.35.refs_0_, bf16[36,64]{1,0:T(8,128)(2,1)} %reshape.36.refs_1_, bf16[3,3,64,64]{3,2,1,0:T(8,128)(2,1)} %refs_2_.5, ...), custom_call_target="tpu_custom_call" | custom-call | tf_op jit(solution)/shard_map/pallas_call | solution.py:729
  52.5 8.2 %all-to-all-done = f32[256,1,128]{2,1,0:T(1,128)S(1)} async-done(((f32[256,1,128]{2,1,0:T(1,128)}), f32[256,1,128]{2,1,0:T(1,128)S(1)}, u32[]{:S(2)}, u32[]{:S(2)}) %all-to-all-start) | async-done | bytes 131104 | tf_op jit(solution)/shard_map/all_to_all | solution.py:774
  60.7 22.4 %shard_map.179 = (f32[256,128]{1,0:T(8,128)}, f32[8,128]{1,0:T(8,128)}, bf16[32,160,128]{2,1,0:T(8,128)(2,1)}, bf16[32,160,128]{2,1,0:T(8,128)(2,1)}, bf16[32,16...) custom-call(s32[3]{0:T(128)S(1)} %pad_add_fusion.refs_0_, ...), custom_call_target="tpu_custom_call" | custom-call | tf_op jit(solution)/shard_map/pallas_call | solution.py:729
  83.1 19.1 %all_to_all.39 = f32[256,1,128]{2,1,0:T(1,128)S(1)} all-to-all(f32[256,1,128]{2,1,0:T(1,128)} %bitcast.22), channel_id=1, replica_groups=mesh['row'=32,'col'=8] {'row','col'}, dimensions={0} | all-to-all | bytes 262144 | tf_op jit(solution)/shard_map/all_to_all | solution.py:774
  103.2 5.5 %all-to-all-start.2 = ((f32[256,1,128]{2,1,0:T(1,128)}), f32[256,1,128]{2,1,0:T(1,128)S(1)}, u32[]{:S(2)}, u32[]{:S(2)}) async-start(f32[256,1,128]{2,1,0:T(1,128)} %reshape.37), calls=%async_computation.2 | async-start | bytes 262144 | tf_op jit(solution)/shard_map/all_to_all | solution.py:774
  108.7 2.8 %shard_map.180 = (bf16[512,768]{1,0:T(8,128)(2,1)}, bf16[512,384]{1,0:T(8,128)(2,1)}, bf16[256,384]{1,0:T(8,128)(2,1)}, bf16[72,128]{1,0:T(8,128)(2,1)}, bf16[96,256]{1,0:T(8,128)(2,1)}) custom-call(bf16[36,128]{1,0:T(8,128)(2,1)} %reshape.35.refs_0_, bf16[36,64]{1,0:T(8,128)(2,1)} %reshape.36.refs_1_, bf16[3,3,64,64]{3,2,1,0:T(8,128)(2,1)} %refs_2_.5, ...), custom_call_target="tpu_custom_call" | custom-call | tf_op jit(solution)/shard_map/pallas_call | solution.py:729
  111.5 0.7 tile.10.refs_2_
  112.3 9.4 %all-to-all-done.2 = f32[256,1,128]{2,1,0:T(1,128)S(1)} async-done(((f32[256,1,128]{2,1,0:T(1,128)}), f32[256,1,128]{2,1,0:T(1,128)S(1)}, u32[]{:S(2)}, u32[]{:S(2)}) %all-to-all-start.2) | async-done | bytes 131104 | tf_op jit(solution)/shard_map/all_to_all | solution.py:774
  121.7 12.6 %shard_map.181 = (bf16[32,128,128]{2,1,0:T(8,128)(2,1)}, f32[256,128]{1,0:T(8,128)}, f32[8,128]{1,0:T(8,128)}) custom-call(s32[3]{0:T(128)S(1)} %pad_add_fusion.refs_0_, f32[256,128]{1,0:T(8,128)S(1)} %bitcast.17, f32[128,128]{1,0:T(8,128)} %tile.10.refs_2_, f32[128,128]{1,0:T(8,128)} %refs_3_.5, bf16[32,160,128]{2,1,0:T(8,128)(2,1)} %get-tuple-element.34.refs_4_, ...), custom_call_target="tpu_custom_call" | custom-call | tf_op jit(solution)/shard_map/pallas_call | solution.py:729
  134.3 5.6 %all-to-all-start.3 = ((f32[256,1,128]{2,1,0:T(1,128)}), f32[256,1,128]{2,1,0:T(1,128)S(1)}, u32[]{:S(2)}, u32[]{:S(2)}) async-start(f32[256,1,128]{2,1,0:T(1,128)} %bitcast.21), calls=%async_computation.3 | async-start | bytes 262144 | tf_op jit(solution)/shard_map/all_to_all | solution.py:774
  139.8 1.2 slice.11
  141.0 11.8 %all-to-all-done.3 = f32[256,1,128]{2,1,0:T(1,128)S(1)} async-done(((f32[256,1,128]{2,1,0:T(1,128)}), f32[256,1,128]{2,1,0:T(1,128)S(1)}, u32[]{:S(2)}, u32[]{:S(2)}) %all-to-all-start.3) | async-done | bytes 131104 | tf_op jit(solution)/shard_map/all_to_all | solution.py:774
  152.8 3.1 %shard_map.182 = bf16[32,128,128]{2,1,0:T(8,128)(2,1)} custom-call(bf16[32,128,128]{2,1,0:T(8,128)(2,1)} %refs_0_.5, bf16[32,128,128]{2,1,0:T(8,128)(2,1)} %get-tuple-element.47.refs_1_, f32[8,128]{1,0:T(8,128)} %get-tuple-element.41.refs_12_.refs_2_, f32[256,128]{1,0:T(8,128)S(1)} %bitcast.19), custom_call_target="tpu_custom_call" | custom-call | tf_op jit(solution)/shard_map/pallas_call | solution.py:729
  (35 shorter events, 3.1 us)
Async XLA Ops:
  1.9 15.0 %collective-permute-start = (bf16[16,128,128]{2,1,0:T(8,128)(2,1)S(1)}, bf16[16,128,128]{2,1,0:T(8,128)(2,1)S(1)}, u32[]{:S(2)}, u32[]{:S(2)}) collective-permute-start(bf16[16,128,128]{2,1,0:T(8,128)(2,1)S(1)} %get-tuple-element.51), channel_id=1, source_target_pairs={{0,8},{8,16},{16,24},{24,32},{32,40},{40,48},{48,56},{56,64},{64,7... | collective-permute-start | bytes 1572872 | tf_op jit(solution)/shard_map/ppermute | solution.py:771
  6.3 41.5 %copy-start.4 = (bf16[3,3,128,3]{2,3,1,0:T(4,128)(2,1)S(1)}, bf16[3,3,128,3]{2,3,1,0:T(4,128)(2,1)}, u32[]{:S(2)}) copy-start(bf16[3,3,128,3]{2,3,1,0:T(4,128)(2,1)} %param.20) | copy-start | bytes 20740
  6.3 42.2 %copy-start.5 = (bf16[3,3,3,64]{3,2,1,0:T(4,128)(2,1)S(1)}, bf16[3,3,3,64]{3,2,1,0:T(4,128)(2,1)}, u32[]{:S(2)}) copy-start(bf16[3,3,3,64]{3,2,1,0:T(4,128)(2,1)} %param.22) | copy-start | bytes 10372
  6.3 14.7 %collective-permute-start.1 = (bf16[16,128,128]{2,1,0:T(8,128)(2,1)S(1)}, bf16[16,128,128]{2,1,0:T(8,128)(2,1)S(1)}, u32[]{:S(2)}, u32[]{:S(2)}) collective-permute-start(bf16[16,128,128]{2,1,0:T(8,128)(2,1)S(1)} %get-tuple-element.50), channel_id=1, source_target_pairs={{8,0},{16,8},{24,16},{32,24},{40,32},{48,40},{56,48},{64,56},{72,6... | collective-permute-start | bytes 1572872 | tf_op jit(solution)/shard_map/ppermute | solution.py:771
  16.9 4.2 %copy-start.1 = (bf16[16,128,128]{2,1,0:T(8,128)(2,1)}, bf16[16,128,128]{2,1,0:T(8,128)(2,1)S(1)}, u32[]{:S(2)}) copy-start(bf16[16,128,128]{2,1,0:T(8,128)(2,1)S(1)} %collective-permute-done.refs_1_.refs_3_) | copy-start | bytes 1572868
  21.1 0.8 copy-start.2
  24.2 27.5 %copy-start.6 = (f32[64]{0:T(128)S(1)}, f32[64]{0:T(128)}, u32[]{:S(2)}) copy-start(f32[64]{0:T(128)} %param.23) | copy-start | bytes 772
  24.2 27.5 %copy-start.7 = (f32[64]{0:T(128)S(1)}, f32[64]{0:T(128)}, u32[]{:S(2)}) copy-start(f32[64]{0:T(128)} %param.25) | copy-start | bytes 772
  24.2 27.5 %copy-start.8 = (f32[128]{0:T(128)S(1)}, f32[128]{0:T(128)}, u32[]{:S(2)}) copy-start(f32[128]{0:T(128)} %param.18) | copy-start | bytes 1540
  24.2 27.5 %copy-start.9 = (f32[128]{0:T(128)S(1)}, f32[128]{0:T(128)}, u32[]{:S(2)}) copy-start(f32[128]{0:T(128)} %param.19) | copy-start | bytes 1540
  24.2 27.5 %copy-start.10 = (f32[128]{0:T(128)S(1)}, f32[128]{0:T(128)}, u32[]{:S(2)}) copy-start(f32[128]{0:T(128)} %param.27) | copy-start | bytes 1540
  24.2 27.5 %copy-start.11 = (f32[128]{0:T(128)S(1)}, f32[128]{0:T(128)}, u32[]{:S(2)}) copy-start(f32[128]{0:T(128)} %param.29) | copy-start | bytes 1540
  24.2 36.5 %copy-start = (f32[3]{0:T(128)S(1)}, f32[3]{0:T(128)}, u32[]{:S(2)}) copy-start(f32[3]{0:T(128)} %refs_1_.1) | copy-start | bytes 40
  24.2 36.4 %collective-permute-start.2 = (bf16[64,16,128]{2,1,0:T(8,128)(2,1)}, bf16[64,16,128]{2,1,0:T(8,128)(2,1)S(1)}, u32[]{:S(2)}, u32[]{:S(2)}) collective-permute-start(bf16[64,16,128]{2,1,0:T(8,128)(2,1)} %get-tuple-element.26), channel_id=1, source_target_pairs={{0,1},{1,2},{2,3},{3,4},{4,5},{5,6},{6,7},{8,9},{9,10},{10,11},{11... | collective-permute-start | bytes 786440 | tf_op jit(solution)/shard_map/ppermute | solution.py:771
  29.1 31.6 %collective-permute-start.3 = (bf16[64,16,128]{2,1,0:T(8,128)(2,1)}, bf16[64,16,128]{2,1,0:T(8,128)(2,1)S(1)}, u32[]{:S(2)}, u32[]{:S(2)}) collective-permute-start(bf16[64,16,128]{2,1,0:T(8,128)(2,1)} %get-tuple-element.27), channel_id=1, source_target_pairs={{1,0},{2,1},{3,2},{4,3},{5,4},{6,5},{7,6},{9,8},{10,9},{11,10},{12... | collective-permute-start | bytes 786440 | tf_op jit(solution)/shard_map/ppermute | solution.py:771
  33.4 27.2 %all-to-all-start = ((f32[256,1,128]{2,1,0:T(1,128)}), f32[256,1,128]{2,1,0:T(1,128)S(1)}, u32[]{:S(2)}, u32[]{:S(2)}) async-start(f32[256,1,128]{2,1,0:T(1,128)} %bitcast.20), calls=%async_computation | async-start | bytes 262144 | tf_op jit(solution)/shard_map/all_to_all | solution.py:774
  83.1 28.4 %copy-start.3 = (f32[64,64]{1,0:T(8,128)S(1)}, f32[64,64]{1,0:T(8,128)}, u32[]{:S(2)}) copy-start(f32[64,64]{1,0:T(8,128)} %param.30) | copy-start | bytes 49156
  103.2 18.5 %all-to-all-start.2 = ((f32[256,1,128]{2,1,0:T(1,128)}), f32[256,1,128]{2,1,0:T(1,128)S(1)}, u32[]{:S(2)}, u32[]{:S(2)}) async-start(f32[256,1,128]{2,1,0:T(1,128)} %reshape.37), calls=%async_computation.2 | async-start | bytes 262144 | tf_op jit(solution)/shard_map/all_to_all | solution.py:774
  134.3 18.5 %all-to-all-start.3 = ((f32[256,1,128]{2,1,0:T(1,128)}), f32[256,1,128]{2,1,0:T(1,128)S(1)}, u32[]{:S(2)}, u32[]{:S(2)}) async-start(f32[256,1,128]{2,1,0:T(1,128)} %bitcast.21), calls=%async_computation.3 | async-start | bytes 262144 | tf_op jit(solution)/shard_map/all_to_all | solution.py:774
